TPU v7x, 32 devices: a whole 2x2x4 slice. The times are simulated.
32 devices in a mesh: groups: 2 (over y), seq: 4 (over z), ep: 2 (over x), tp: 2 (over core).
Axes of the slice: x: 2, y: 2, z: 4, core: 2. Of those that a mesh axis runs over, the one named last changes fastest.
Arguments:
- hidden: bfloat16 [2048, 1440], P(('groups', 'seq', 'ep')), parts along dimension 0, may hold values from -6 to 6
- expert_ids: int32 [2048, 4], P(('groups', 'seq', 'ep')), parts along dimension 0, may hold values from 0 to 7, all different within a row; in each aligned block of 128 rows (0 to 127, 128 to 255, ...) at most 88 rows name the same one
- gate_units: int32 [2048, 4], P(('groups', 'seq', 'ep')), parts along dimension 0, may hold values from 4096 to 32767
- w_gate: bfloat16 [8, 1440, 1440], P(('seq', 'tp'), None, 'ep'), may hold values from -0.15625 to 0.15625
- w_up: bfloat16 [8, 1440, 1440], P(('seq', 'tp'), None, 'ep'), may hold values from -0.15625 to 0.15625
- w_down: bfloat16 [8, 1440, 1440], P(('seq', 'tp'), None, 'ep'), may hold values from -0.15625 to 0.15625
Outputs:
- moe_out: bfloat16 [2048, 1440], P(('groups', 'seq', 'ep'), 'tp'), parts along dimension 0
There are 2 independent parts, one for each index of `groups`. A program takes and returns all parts, laid end to end along the dimension named above; an argument that names none is the same for every part. Nothing has to cross between parts.
Inputs may be any that keep to these rules, and one draw needn't show every extreme that they name: `expert_ids`: each row names 4 different experts; in each aligned block of 128 rows no expert is named by more than 88 rows, and in every draw some expert is named by exactly 88 rows of some block.
All inputs are finite; a program needn't handle non-finite values.
Results may differ from a plain program's by a relative error of at most 0.0064.
Values may be sent and summed in bfloat16 or wider, within the bound.
A program may use at most 64 MiB of HBM per device.

v0:
```python
import jax
import jax.numpy as jnp
from jax import lax
from jax.sharding import PartitionSpec as P

TOP = 4


def slice_output(rows_in, gate_cols, up_cols, down_cols):
    gate_pre = jnp.dot(rows_in, gate_cols, preferred_element_type=jnp.float32)
    up_pre = jnp.dot(rows_in, up_cols, preferred_element_type=jnp.float32)
    activation = ((up_pre + 1.0) * gate_pre * jax.nn.sigmoid(1.702 * gate_pre)).astype(jnp.bfloat16)
    return lax.dot_general(
        activation, down_cols, (((1,), (1,)), ((), ())), preferred_element_type=jnp.float32
    ).astype(jnp.bfloat16)


def local(hidden, expert_ids, gate_units, w_gate, w_up, w_down):
    token_count, model_width = hidden.shape
    seq_count = lax.axis_size("seq")
    ep_count = lax.axis_size("ep")
    tp_count = lax.axis_size("tp")
    half_width = model_width // tp_count
    my_half = lax.axis_index("tp")
    expert_count = seq_count * tp_count
    capacity = max(2, (token_count * TOP * 11 + expert_count * 8 - 1) // (expert_count * 8))
    flat_ids = expert_ids.reshape(-1)
    onehot_ids = (flat_ids[:, None] == jnp.arange(expert_count, dtype=jnp.int32)[None, :]).astype(
        jnp.int32
    )
    slot_rank = jnp.sum((jnp.cumsum(onehot_ids, axis=0) - 1) * onehot_ids, axis=1)
    owner_seq = flat_ids // tp_count
    owner_half = flat_ids % tp_count
    send_row = jnp.where(owner_half == my_half, owner_seq * capacity + slot_rank, -1)
    selector = jnp.arange(seq_count * capacity, dtype=jnp.int32)[:, None] == send_row[None, :]
    selector = jnp.any(selector.reshape(seq_count * capacity, token_count, TOP), axis=2).astype(
        jnp.bfloat16
    )
    outgoing = jnp.dot(selector, hidden, preferred_element_type=jnp.float32).astype(jnp.bfloat16)
    outgoing = outgoing.reshape(seq_count, capacity, model_width)
    column_of = (owner_half * seq_count + owner_seq) * capacity + slot_rank
    gate_share = gate_units.reshape(-1).astype(jnp.float32) / 65536.0
    column_ids = jnp.arange(tp_count * seq_count * capacity, dtype=jnp.int32)
    combiner = jnp.where(column_ids[None, :] == column_of[:, None], gate_share[:, None], 0.0)
    combiner = jnp.sum(combiner.reshape(token_count, TOP, -1), axis=1)
    copied = jnp.broadcast_to(outgoing[:, None], (seq_count, ep_count, capacity, model_width))
    copied = copied.reshape(seq_count * ep_count, capacity, model_width)
    arrived = lax.all_to_all(copied, ("seq", "ep"), split_axis=0, concat_axis=0, tiled=True)
    slice_rows = slice_output(arrived.reshape(-1, model_width), w_gate[0], w_up[0], w_down[0])
    slice_rows = slice_rows.reshape(seq_count * ep_count, capacity, model_width)
    came_back = lax.all_to_all(
        lax.all_to_all(slice_rows, ("seq", "ep"), split_axis=0, concat_axis=0, tiled=True),
        "tp",
        split_axis=2,
        concat_axis=0,
        tiled=True,
    )
    came_back = came_back.reshape(tp_count, seq_count, ep_count, capacity, half_width)
    returned = jnp.sum(came_back.astype(jnp.float32), axis=2).astype(jnp.bfloat16)
    result_rows = returned.reshape(-1, half_width).astype(jnp.float32)
    moe_out = jnp.dot(
        combiner, result_rows, precision=lax.Precision.HIGHEST, preferred_element_type=jnp.float32
    )
    return moe_out.astype(jnp.bfloat16)


def solution(mesh):
    return jax.shard_map(
        local,
        mesh=mesh,
        in_specs=(
            P(("groups", "seq", "ep"), None),
            P(("groups", "seq", "ep"), None),
            P(("groups", "seq", "ep"), None),
            P(("seq", "tp"), None, "ep"),
            P(("seq", "tp"), None, "ep"),
            P(("seq", "tp"), None, "ep"),
        ),
        out_specs=P(("groups", "seq", "ep"), "tp"),
        check_vma=False,
    )
```

profile of v0, /device:TPU:0, one launch (start us, length us, event | category | flops | bytes accessed | tf_op | source)
XLA Modules:
  0.0 157.3 jit_solution(9115896044357004231)
XLA Ops:
  0.0 0.0 copy-start
  0.0 0.9 copy.72
  0.9 0.1 eq.70
  1.0 0.1 eq.66
  1.2 1.1 reduce-window.6
  2.3 0.2 slice_reduce_fusion
  2.6 0.1 fusion.10
  2.7 0.1 reduce_sum.33
  2.8 0.1 copy.74
  2.8 0.7 add_select_fusion.2
  3.6 0.1 fusion.9
  3.7 1.4 convolution_convert_fusion.1
  5.1 0.2 broadcast_in_dim.30
  5.3 0.0 copy-start.3
  5.3 57.4 %all_to_all.25 = bf16[8,88,1440]{2,1,0:T(8,128)(2,1)S(1)} all-to-all(bf16[8,88,1440]{2,1,0:T(8,128)(2,1)S(1)} %bitcast.36), channel_id=1, replica_groups=mesh['groups'=2,'seq'=4,'ep'=2,'tp'=2] {'seq','ep'}, dimensions={0} | all-to-all | bytes 4055040 | tf_op jit(solution)/shard_map/all_to_all | solution.py:48
  62.7 0.0 copy-start.1
  62.7 1.3 copy-done.1
  64.1 0.0 copy-done.3
  64.1 3.2 %fusion.1 = f32[704,720]{1,0:T(8,128)} fusion(bf16[704,1440]{1,0:T(8,128)(2,1)S(1)} %bitcast.40, bf16[1,1440,720]{2,1,0:T(8,128)(2,1)S(1)} %copy-done.3), kind=kOutput, calls=%fused_computation.3 | convolution fusion | flops 1459814400 | bytes 6128640 | tf_op jit(solution)/shard_map/dot_general | solution.py:10
  67.2 0.0 copy-done
  67.2 8.6 %convolution_convert_fusion = bf16[704,1440]{1,0:T(8,128)(2,1)} fusion(bf16[1,1440,720]{2,1,0:T(8,128)(2,1)S(1)} %copy-done, f32[704,720]{1,0:T(8,128)} %fusion.1, bf16[704,1440]{1,0:T(8,128)(2,1)} %bitcast.41, bf16[1,1440,720]{2,1,0:T(8,128)(2,1)} %param.10), kind=kOutput, calls=%fused_computation | convolution fusion | flops 2924697600 | bytes 10229760 | tf_op jit(solution)/shard_map/dot_general | solution.py:13
  75.8 0.0 copy-start.2
  75.8 4.5 %all-to-all-start.1 = ((bf16[8,88,1440]{2,1,0:T(8,128)(2,1)}), bf16[8,88,1440]{2,1,0:T(8,128)(2,1)}, u32[]{:S(2)}, u32[]{:S(2)}) async-start(bf16[8,88,1440]{2,1,0:T(8,128)(2,1)} %bitcast.39), calls=%async_computation.1 | async-start | bytes 4325376 | tf_op jit(solution)/shard_map/all_to_all | solution.py:52
  80.3 0.0 copy-done.2
  80.3 0.2 select_reduce_fusion
  80.5 48.5 %all-to-all-done.1 = bf16[8,88,1440]{2,1,0:T(8,128)(2,1)} async-done(((bf16[8,88,1440]{2,1,0:T(8,128)(2,1)}), bf16[8,88,1440]{2,1,0:T(8,128)(2,1)}, u32[]{:S(2)}, u32[]{:S(2)}) %all-to-all-start.1) | async-done | bytes 2027552 | tf_op jit(solution)/shard_map/all_to_all | solution.py:52
  129.0 4.7 %copy.76 = bf16[8,88,1440]{1,0,2:T(8,128)(2,1)} copy(bf16[8,88,1440]{2,1,0:T(8,128)(2,1)} %all-to-all-done.1) | data formatting | bytes 4055040 | tf_op jit(solution)/shard_map/all_to_all | solution.py:52
  133.8 10.1 %all_to_all.26 = bf16[8,88,1440]{1,0,2:T(8,128)(2,1)} all-to-all(bf16[8,88,1440]{1,0,2:T(8,128)(2,1)} %copy.76), channel_id=1, replica_groups=mesh['groups'=2,'seq'=4,'ep'=2,'tp'=2] {'tp'}, dimensions={2} | all-to-all | bytes 4055040 | tf_op jit(solution)/shard_map/all_to_all | solution.py:51
  143.8 6.2 %copy.77 = bf16[2,8,88,720]{3,0,2,1:T(2,128)(2,1)} copy(bf16[2,8,88,720]{2,1,3,0:T(8,128)(2,1)} %bitcast.35) | data formatting | bytes 4055040 | tf_op jit(solution)/shard_map/all_to_all | solution.py:51
  150.0 5.2 %bitcast_reduce_fusion = bf16[2,4,88,720]{3,0,2,1:T(2,128)(2,1)S(1)} fusion(bf16[2,8,88,720]{3,0,2,1:T(2,128)(2,1)} %copy.77), kind=kLoop, calls=%fused_computation.7 | loop fusion | flops 506880 | bytes 3041280 | tf_op jit(solution)/shard_map/reduce_sum | solution.py:59
  155.2 0.1 copy.78
  155.3 2.0 %convolution_convert_fusion.2 = bf16[128,720]{0,1:T(8,128)(2,1)} fusion(f32[128,704]{0,1:T(8,128)S(1)} %select_reduce_fusion, bf16[704,720]{1,0:T(8,128)(2,1)S(1)} %bitcast.37), kind=kOutput, calls=%fused_computation.11 | convolution fusion | flops 778659840 | bytes 1558528 | tf_op jit(solution)/shard_map/dot_general | solution.py:61
  (4 shorter events, 0.0 us)
Async XLA Ops:
  0.0 67.2 %copy-start = (bf16[1,1440,720]{2,1,0:T(8,128)(2,1)S(1)}, bf16[1,1440,720]{2,1,0:T(8,128)(2,1)}, u32[]{:S(2)}) copy-start(bf16[1,1440,720]{2,1,0:T(8,128)(2,1)} %param.11) | copy-start | bytes 6220804
  5.3 58.8 %copy-start.3 = (bf16[1,1440,720]{2,1,0:T(8,128)(2,1)S(1)}, bf16[1,1440,720]{2,1,0:T(8,128)(2,1)}, u32[]{:S(2)}) copy-start(bf16[1,1440,720]{2,1,0:T(8,128)(2,1)} %param.9) | copy-start | bytes 6220804
  62.7 1.3 copy-start.1
  75.8 4.5 %copy-start.2 = (s32[128,4]{0,1:T(4,128)S(1)}, s32[128,4]{0,1:T(4,128)}, u32[]{:S(2)}) copy-start(s32[128,4]{0,1:T(4,128)} %param.8) | copy-start | bytes 6148
  75.8 53.2 %all-to-all-start.1 = ((bf16[8,88,1440]{2,1,0:T(8,128)(2,1)}), bf16[8,88,1440]{2,1,0:T(8,128)(2,1)}, u32[]{:S(2)}, u32[]{:S(2)}) async-start(bf16[8,88,1440]{2,1,0:T(8,128)(2,1)} %bitcast.39), calls=%async_computation.1 | async-start | bytes 4325376 | tf_op jit(solution)/shard_map/all_to_all | solution.py:52
where the time goes:
time: 158 us; the launch traced here: 157 us
  blocking collectives  67.5 us (43%)
  waiting for transfers between devices  48.5 us (31%)
  matrix products  15.2 us (10%)
  local copies, waits for them, and re-layouts  14.1 us (9%)
  other arithmetic  7.45 us (5%)
  starting transfers between devices  4.5 us (3%)
    all_to_all x1, blocking collectives, local(): lax.all_to_all(copied, ('seq', 'ep'), split_axis=0, concat_axis=0, tiled=...  57.4 us
    all_to_all x1, waiting for transfers between devices, local(): lax.all_to_all(slice_rows, ('seq', 'ep'), split_axis=0, concat_axis=0, ti...  48.5 us
    all_to_all x1, blocking collectives, local(): lax.all_to_all(lax.all_to_all(slice_rows, ('seq', 'ep'), split_axis=0, co...  10.1 us
    dot_general x1, matrix products, slice_output(): lax.dot_general(activation, down_cols, (((1,), (1,)), ((), ())), preferre...  8.55 us
    all_to_all x1, local copies, waits for them, and re-layouts, local(): lax.all_to_all(lax.all_to_all(slice_rows, ('seq', 'ep'), split_axis=0, co...  6.16 us
    reduce_sum x1, other arithmetic, local(): jnp.sum(came_back.astype(jnp.float32), axis=2).astype(jnp.bfloat16)  5.2 us
    all_to_all x1, local copies, waits for them, and re-layouts, local(): lax.all_to_all(slice_rows, ('seq', 'ep'), split_axis=0, concat_axis=0, ti...  4.73 us
    all_to_all x1, starting transfers between devices, local(): lax.all_to_all(slice_rows, ('seq', 'ep'), split_axis=0, concat_axis=0, ti...  4.5 us
  transfers between devices with their start and end apart: 1, of which 1 were waited for; matrix products, arithmetic and copies ran while one was open for 0% of the time, Pallas kernels for 0%

commit v1 on v0

--- a/solution.py
+++ b/solution.py
@@ -1,6 +1,10 @@
+import functools
+
 import jax
 import jax.numpy as jnp
 from jax import lax
+from jax.experimental import pallas as pl
+from jax.experimental.pallas import tpu as pltpu
 from jax.sharding import PartitionSpec as P
 
 TOP = 4
@@ -15,7 +19,7 @@
     ).astype(jnp.bfloat16)
 
 
-def local(hidden, expert_ids, gate_units, w_gate, w_up, w_down):
+def routed(hidden, expert_ids, gate_units, w_gate, w_up, w_down):
     token_count, model_width = hidden.shape
     seq_count = lax.axis_size("seq")
     ep_count = lax.axis_size("ep")
@@ -64,6 +68,224 @@
     return moe_out.astype(jnp.bfloat16)
 
 
+LANES = 128
+MESH = pl.DeviceIdType.MESH
+
+
+def gather_kernel(
+    seq_count, hidden_ref, ids_ref, units_ref, gate_hbm, up_hbm, down_hbm, out_ref,
+    tokens, gate_w, up_w, down_w, mine, other, other_in, across, across_in, along, along_in,
+    load_sem, gz_send, gz_recv, gx_send, gx_recv, gp_send, gp_recv,
+    rp_send, rp_recv, rx_send, rx_recv, rz_send, rz_recv,
+):
+    seq, ep, tp = lax.axis_index("seq"), lax.axis_index("ep"), lax.axis_index("tp")
+    rows, width = hidden_ref.shape
+    half_rows = rows // 2
+    half_width = out_ref.shape[1]
+    padded = tokens.shape[2]
+    expert_count = seq_count * 2
+    side, core = {"ep": 1 - ep}, {"tp": 1 - tp}
+
+    def ahead(step):
+        return {"seq": lax.rem(seq + step, seq_count)}
+
+    def behind(step):
+        return {"seq": lax.rem(seq + seq_count - step, seq_count)}
+
+    barrier = pltpu.get_barrier_semaphore()
+    for peer in [side, core] + [ahead(step) for step in range(1, seq_count)]:
+        pl.semaphore_signal(barrier, inc=1, device_id=peer, device_id_type=MESH)
+
+    loads = [
+        pltpu.make_async_copy(gate_hbm.at[0], gate_w.at[pl.ds(0, width)], load_sem.at[0]),
+        pltpu.make_async_copy(up_hbm.at[0], up_w.at[pl.ds(0, width)], load_sem.at[1]),
+        pltpu.make_async_copy(down_hbm.at[0], down_w, load_sem.at[2]),
+    ]
+    for load in loads:
+        load.start()
+
+    tail = width // LANES * LANES
+    spare = width - tail
+    tokens[0, 0:rows, 0:tail] = hidden_ref[:, 0:tail]
+    lane = lax.broadcasted_iota(jnp.int32, (rows, LANES), 1)
+    ids, units = ids_ref[...], units_ref[...]
+    parts = jnp.zeros((rows, LANES), jnp.int32)
+    for choice in range(TOP):
+        expert = ids[:, choice : choice + 1]
+        unit = units[:, choice : choice + 1]
+        parts += jnp.where(lane == expert + spare, unit // 256, 0)
+        parts += jnp.where(lane == expert + (spare + expert_count), unit % 256, 0)
+    tokens[0, 0:rows, tail:padded] = parts.astype(jnp.float32).astype(jnp.bfloat16)
+    tokens[0, 0:rows, tail:width] = hidden_ref[:, tail:width]
+    zeros = jnp.zeros((padded - width, gate_w.shape[1]), jnp.bfloat16)
+    gate_w[width:padded, :] = zeros
+    up_w[width:padded, :] = zeros
+
+    pl.semaphore_wait(barrier, seq_count + 1)
+
+    my_rows = pl.ds(pl.multiple_of(tp * half_rows, half_rows), half_rows)
+    my_far_rows = pl.ds(pl.multiple_of(rows + tp * half_rows, half_rows), half_rows)
+    sends = []
+
+    def send(src, dst, send_sem, recv_sem, peer):
+        copy = pltpu.make_async_remote_copy(
+            src_ref=src, dst_ref=dst, send_sem=send_sem, recv_sem=recv_sem,
+            device_id=peer, device_id_type=MESH,
+        )
+        copy.start()
+        sends.append(copy)
+        return copy
+
+    z_in, x_in, p_in = {}, {}, {}
+
+    def forward_across(step):
+        x_in[step] = send(
+            tokens.at[step, my_rows], tokens.at[step, my_far_rows],
+            gx_send.at[step], gx_recv.at[step], side,
+        )
+
+    forward_across(0)
+    for step in range(1, seq_count):
+        z_in[step] = send(
+            tokens.at[0, my_rows], tokens.at[step, my_rows],
+            gz_send.at[step], gz_recv.at[step], ahead(step),
+        )
+
+    def to_core(step, far):
+        where = my_far_rows if far else my_rows
+        p_in[step, far] = send(
+            tokens.at[step, where], tokens.at[step, where],
+            gp_send.at[2 * step + far], gp_recv.at[2 * step + far], core,
+        )
+
+    def gather(step):
+        if step > 0:
+            z_in[step].wait_recv()
+            forward_across(step)
+            to_core(step, 0)
+        x_in[step].wait_recv()
+        to_core(step, 1)
+        if step > 0:
+            p_in[step, 0].wait_recv()
+        p_in[step, 1].wait_recv()
+
+    my_expert = seq * 2 + tp
+    lanes = lax.broadcasted_iota(jnp.int32, (1, LANES), 1)
+    picker = jnp.where(lanes == my_expert + spare, 256.0 / 65536.0, 0.0)
+    picker += jnp.where(lanes == my_expert + (spare + expert_count), 1.0 / 65536.0, 0.0)
+    r_in, rx_in, rz_in = {}, {}, {}
+
+    def down_part(activation, which):
+        cols = down_w[pl.ds(pl.multiple_of(which * half_width, 16), half_width), :]
+        return lax.dot_general(
+            activation, cols, (((1,), (1,)), ((), ())), preferred_element_type=jnp.float32
+        )
+
+    def compute(step):
+        rows_in = tokens[step]
+        gate_pre = jnp.dot(rows_in, gate_w[...], preferred_element_type=jnp.float32)
+        up_pre = jnp.dot(rows_in, up_w[...], preferred_element_type=jnp.float32)
+        activation = ((up_pre + 1.0) * gate_pre * jax.nn.sigmoid(1.702 * gate_pre)).astype(jnp.bfloat16)
+        share = tokens[step, :, tail:padded].astype(jnp.float32)
+        share = jnp.sum(share * picker, axis=1, keepdims=True)
+        other[step] = (down_part(activation, 1 - tp) * share).astype(jnp.bfloat16)
+        r_in[step] = send(
+            other.at[step], other_in.at[step], rp_send.at[step], rp_recv.at[step], core
+        )
+        mine[step] = down_part(activation, tp) * share
+
+    def join_cores(step):
+        r_in[step].wait_recv()
+        across[step] = (
+            mine[step, rows:, :] + other_in[step, rows:, :].astype(jnp.float32)
+        ).astype(jnp.bfloat16)
+        rx_in[step] = send(
+            across.at[step], across_in.at[step], rx_send.at[step], rx_recv.at[step], side
+        )
+
+    def join_sides(step):
+        rx_in[step].wait_recv()
+        total = mine[step, 0:rows, :] + other_in[step, 0:rows, :].astype(jnp.float32)
+        total += across_in[step].astype(jnp.float32)
+        if step == 0:
+            mine[0, 0:rows, :] = total
+        else:
+            along[step] = total.astype(jnp.bfloat16)
+            rz_in[step] = send(
+                along.at[step], along_in.at[step], rz_send.at[step], rz_recv.at[step], behind(step)
+            )
+
+    for step in range(seq_count + 2):
+        if step < seq_count:
+            gather(step)
+            if step == 0:
+                for load in loads:
+                    load.wait()
+            compute(step)
+        if 1 <= step <= seq_count:
+            join_cores(step - 1)
+        if step >= 2:
+            join_sides(step - 2)
+
+    total = mine[0, 0:rows, :]
+    for step in range(1, seq_count):
+        rz_in[step].wait_recv()
+        total += along_in[step].astype(jnp.float32)
+    out_ref[...] = total.astype(jnp.bfloat16)
+    for copy in sends:
+        copy.wait_send()
+
+
+def gathered(hidden, expert_ids, gate_units, w_gate, w_up, w_down):
+    rows, width = hidden.shape
+    units = w_gate.shape[2]
+    seq_count = lax.axis_size("seq")
+    half = width // 2
+    padded = -(-width // LANES) * LANES
+    vmem = pl.BlockSpec(memory_space=pltpu.VMEM)
+    hbm = pl.BlockSpec(memory_space=pl.ANY)
+    dma = pltpu.SemaphoreType.DMA
+    sems = [dma((seq_count,))] * 2
+    return pl.pallas_call(
+        functools.partial(gather_kernel, seq_count),
+        out_shape=jax.ShapeDtypeStruct((rows, half), jnp.bfloat16),
+        in_specs=[vmem] * 3 + [hbm] * 3,
+        out_specs=vmem,
+        scratch_shapes=[
+            pltpu.VMEM((seq_count, 2 * rows, padded), jnp.bfloat16),
+            pltpu.VMEM((padded, units), jnp.bfloat16),
+            pltpu.VMEM((padded, units), jnp.bfloat16),
+            pltpu.VMEM((width, units), jnp.bfloat16),
+            pltpu.VMEM((seq_count, 2 * rows, half), jnp.float32),
+            pltpu.VMEM((seq_count, 2 * rows, half), jnp.bfloat16),
+            pltpu.VMEM((seq_count, 2 * rows, half), jnp.bfloat16),
+            pltpu.VMEM((seq_count, rows, half), jnp.bfloat16),
+            pltpu.VMEM((seq_count, rows, half), jnp.bfloat16),
+            pltpu.VMEM((seq_count, rows, half), jnp.bfloat16),
+            pltpu.VMEM((seq_count, rows, half), jnp.bfloat16),
+            dma((3,)),
+        ]
+        + sems * 2
+        + [dma((2 * seq_count,))] * 2
+        + sems * 3,
+        compiler_params=pltpu.CompilerParams(
+            collective_id=0, has_side_effects=True, vmem_limit_bytes=60 * 1024 * 1024
+        ),
+    )(hidden, expert_ids, gate_units, w_gate, w_up, w_down)
+
+
+def local(hidden, expert_ids, gate_units, w_gate, w_up, w_down):
+    token_count, model_width = hidden.shape
+    seq_count = lax.axis_size("seq")
+    expert_count = seq_count * lax.axis_size("tp")
+    spare = -model_width % LANES
+    pairs = lax.axis_size("ep") == 2 and lax.axis_size("tp") == 2
+    whole_blocks = 2 * token_count * TOP * 11 >= expert_count * 8 * token_count
+    if pairs and whole_blocks and 2 * expert_count <= spare:
+        return gathered(hidden, expert_ids, gate_units, w_gate, w_up, w_down)
+    return routed(hidden, expert_ids, gate_units, w_gate, w_up, w_down)
+
+
 def solution(mesh):
     return jax.shard_map(
         local,

time: 158 us -> 83.2 us (0.53)
  Pallas kernels: 0 us -> 76.5 us
  blocking collectives: 67.5 us -> 0 us
  waiting for transfers between devices: 48.5 us -> 0 us
  matrix products: 15.2 us -> 0 us
  local copies, waits for them, and re-layouts: 14.1 us -> 6.45 us
  other arithmetic: 7.45 us -> 0 us
  starting transfers between devices: 4.5 us -> 0 us
    pallas_call x0 -> x1, Pallas kernels: none -> 76.5 us  [gathered(): pl.pallas_call(functools.partial(gather_kernel, seq_count), out_shape=jax...]
    all_to_all x2 -> x0, blocking collectives: 67.5 us -> none  [the longest x1 57.4 us: local(): lax.all_to_all(copied, ('seq', 'ep'), split_axis=0, concat_axis=0, tiled=...]
    all_to_all x1 -> x0, waiting for transfers between devices: 48.5 us -> none  [local(): lax.all_to_all(slice_rows, ('seq', 'ep'), split_axis=0, concat_axis=0, ti...]
    dot_general x4 -> x0, matrix products: 15.2 us -> none  [the longest x1 8.55 us: slice_output(): lax.dot_general(activation, down_cols, (((1,), (1,)), ((), ())), preferre...]
    all_to_all x2 -> x0, local copies, waits for them, and re-layouts: 10.9 us -> none  [the longest x1 6.16 us: local(): lax.all_to_all(lax.all_to_all(slice_rows, ('seq', 'ep'), split_axis=0, co...]
    reduce_sum x3 -> x0, other arithmetic: 5.46 us -> none  [the longest x1 5.2 us: local(): jnp.sum(came_back.astype(jnp.float32), axis=2).astype(jnp.bfloat16)]
    all_to_all x1 -> x0, starting transfers between devices: 4.5 us -> none  [local(): lax.all_to_all(slice_rows, ('seq', 'ep'), split_axis=0, concat_axis=0, ti...]
    unnamed x9 -> x3, local copies, waits for them, and re-layouts: 2.3 us -> 4.72 us
  transfers between devices with their start and end apart: 1 -> 0, of which waited for: 1 -> 0; matrix products, arithmetic and copies ran while one was open for 0% -> 0% of each run, Pallas kernels for 0% -> 0%
where the time goes in v1:
time: 83.2 us; the launch traced here: 83 us
  Pallas kernels  76.5 us (92%)
  local copies, waits for them, and re-layouts  6.45 us (8%)
    pallas_call x1, Pallas kernels, gathered(): pl.pallas_call(functools.partial(gather_kernel, seq_count), out_shape=jax...  76.5 us
    unnamed x3, local copies, waits for them, and re-layouts  4.72 us
    pallas_call x1, local copies, waits for them, and re-layouts, gathered(): pl.pallas_call(functools.partial(gather_kernel, seq_count), out_shape=jax...  1.74 us

profile of v1, /device:TPU:0, one launch (start us, length us, event | category | flops | bytes accessed | tf_op | source)
XLA Modules:
  0.0 83.0 jit_solution(14916267628333288541)
XLA Ops:
  0.0 1.4 %copy.8.ids_ref = s32[128,4]{1,0:T(8,128)} copy(s32[128,4]{0,1:T(4,128)} %param.7) | data formatting | bytes 4096 | tf_op args[1]
  1.4 1.4 %copy.9.units_ref = s32[128,4]{1,0:T(8,128)} copy(s32[128,4]{0,1:T(4,128)} %param.8) | data formatting | bytes 4096 | tf_op args[2]
  2.8 1.9 %copy.7.hidden_ref = bf16[128,1440]{1,0:T(8,128)(2,1)} copy(bf16[128,1440]{0,1:T(8,128)(2,1)} %param.6) | data formatting | bytes 737280 | tf_op args[0]
  4.7 76.5 %shard_map.64 = bf16[128,720]{1,0:T(8,128)(2,1)} custom-call(bf16[128,1440]{1,0:T(8,128)(2,1)} %copy.7.hidden_ref, s32[128,4]{1,0:T(8,128)} %copy.8.ids_ref, s32[128,4]{1,0:T(8,128)} %copy.9.units_ref, bf16[1,1440,720]{2,1,0:T(8,128)(2,1)} %gate_hbm.1, bf16[1,1440,720]{2,1,0:T(8,128)(2,1)} %up_hbm.1, bf16[1,1440,720]{2,1,0:T(8,128)(2,1)} %down_hbm.1), custom_call_target="tpu_custom_call" | custom-call | tf_op jit(solution)/shard_map/pallas_call | solution.py:249
  81.2 1.7 %copy.10 = bf16[128,720]{0,1:T(8,128)(2,1)} copy(bf16[128,720]{1,0:T(8,128)(2,1)} %shard_map.64) | data formatting | bytes 368640 | tf_op jit(solution)/shard_map/pallas_call | solution.py:249

commit v2 on v0

--- a/solution.py
+++ b/solution.py
@@ -1,6 +1,10 @@
+import functools
+
 import jax
 import jax.numpy as jnp
 from jax import lax
+from jax.experimental import pallas as pl
+from jax.experimental.pallas import tpu as pltpu
 from jax.sharding import PartitionSpec as P
 
 TOP = 4
@@ -15,7 +19,7 @@
     ).astype(jnp.bfloat16)
 
 
-def local(hidden, expert_ids, gate_units, w_gate, w_up, w_down):
+def routed(hidden, expert_ids, gate_units, w_gate, w_up, w_down):
     token_count, model_width = hidden.shape
     seq_count = lax.axis_size("seq")
     ep_count = lax.axis_size("ep")
@@ -64,6 +68,262 @@
     return moe_out.astype(jnp.bfloat16)
 
 
+LANES = 128
+MESH = pl.DeviceIdType.MESH
+
+
+def gather_kernel(
+    seq_count, hidden_ref, ids_ref, units_ref, gate_hbm, up_hbm, down_hbm, out_ref,
+    tokens, gate_w, up_w, down_w, mine, other, other_in, across, across_in, along, along_in, final,
+    load_sem, gx_send, gx_recv, rp_send, rp_recv, rx_send, rx_recv, rz_send, rz_recv,
+    gp_send, gp_recv, gz_send, gz_recv,
+):
+    seq, ep, tp = lax.axis_index("seq"), lax.axis_index("ep"), lax.axis_index("tp")
+    width, rows = hidden_ref.shape
+    half_rows = rows // 2
+    half_width = out_ref.shape[0]
+    padded = tokens.shape[2]
+    expert_count = seq_count * 2
+    last = seq_count - 1
+    side, core = {"ep": 1 - ep}, {"tp": 1 - tp}
+
+    barrier = pltpu.get_barrier_semaphore()
+    around = [{"seq": lax.rem(seq + step, seq_count)} for step in range(1, seq_count)]
+    for peer in [side, core] + around:
+        pl.semaphore_signal(barrier, inc=1, device_id=peer, device_id_type=MESH)
+
+    loads = [
+        pltpu.make_async_copy(gate_hbm.at[0], gate_w.at[pl.ds(0, width)], load_sem.at[0]),
+        pltpu.make_async_copy(up_hbm.at[0], up_w.at[pl.ds(0, width)], load_sem.at[1]),
+        pltpu.make_async_copy(down_hbm.at[0], down_w, load_sem.at[2]),
+    ]
+    for load in loads:
+        load.start()
+
+    tail = width // LANES * LANES
+    first = width - tail
+    slot = lax.broadcasted_iota(jnp.int32, (LANES, rows), 0)
+    parts = jnp.zeros((LANES, rows), jnp.int32)
+    for choice in range(TOP):
+        expert = ids_ref[choice : choice + 1, :]
+        unit = units_ref[choice : choice + 1, :]
+        parts += jnp.where(slot == expert + first, unit // 256, 0)
+        parts += jnp.where(slot == expert + (first + expert_count), unit % 256, 0)
+    parts = parts.astype(jnp.float32)
+    if first:
+        rest = hidden_ref[tail:width, :].astype(jnp.float32)
+        parts += jnp.concatenate([rest, jnp.zeros((LANES - first, rows), jnp.float32)], axis=0)
+    tokens[seq, 0:rows, tail:padded] = parts.T.astype(jnp.bfloat16)
+    for low in range(0, tail, LANES):
+        piece = hidden_ref[low : low + LANES, :].astype(jnp.float32)
+        tokens[seq, 0:rows, low : low + LANES] = piece.T.astype(jnp.bfloat16)
+    zeros = jnp.zeros((padded - width, gate_w.shape[1]), jnp.bfloat16)
+    gate_w[width:padded, :] = zeros
+    up_w[width:padded, :] = zeros
+
+    pl.semaphore_wait(barrier, seq_count + 1)
+
+    my_rows = pl.ds(pl.multiple_of(tp * half_rows, half_rows), half_rows)
+    my_far_rows = pl.ds(pl.multiple_of(rows + tp * half_rows, half_rows), half_rows)
+    sends = []
+
+    def describe(src, dst, send_sem, recv_sem, peer):
+        return pltpu.make_async_remote_copy(
+            src_ref=src, dst_ref=dst, send_sem=send_sem, recv_sem=recv_sem,
+            device_id=peer, device_id_type=MESH,
+        )
+
+    def send(*parts, when=None):
+        if when is None:
+            copy = describe(*parts)
+            copy.start()
+            sends.append((copy, None, None))
+            return copy
+
+        @pl.when(when)
+        def _():
+            describe(*parts).start()
+
+        sends.append((None, parts, when))
+
+    short = jnp.minimum(seq, last - seq)
+    blocks, signs = [seq], [None]
+    for event in range(1, seq_count):
+        paired = event <= 2 * short
+        sign = jnp.where(paired, 1 - 2 * (event % 2), jnp.where(seq < last - seq, 1, -1))
+        distance = jnp.where(paired, (event + 1) // 2, event - short)
+        blocks.append(seq + sign * distance)
+        signs.append(sign)
+
+    x_in, p_in, r_in, rx_in = {}, {}, {}, {}
+
+    def block_along(event, sem, onward, when):
+        block = blocks[event]
+        where = tokens.at[block, my_rows]
+        send(where, where, gz_send.at[sem], gz_recv.at[block], {"seq": onward}, when=when)
+
+    def block_across(event):
+        block = blocks[event]
+        x_in[event] = send(
+            tokens.at[block, my_rows], tokens.at[block, my_far_rows],
+            gx_send.at[event], gx_recv.at[event], side,
+        )
+
+    def to_core(event, far):
+        where = tokens.at[blocks[event], my_far_rows if far else my_rows]
+        p_in[event, far] = send(
+            where, where, gp_send.at[2 * event + far], gp_recv.at[2 * event + far], core
+        )
+
+    def arrive(event):
+        block = blocks[event]
+        where = tokens.at[block, my_rows]
+        describe(where, where, gz_send.at[event], gz_recv.at[block], side).wait_recv()
+        onward = seq - signs[event]
+        inside = jnp.logical_and(onward >= 0, onward <= last)
+        block_along(event, event, jnp.clip(onward, 0, last), inside)
+        block_across(event)
+        to_core(event, 0)
+
+    my_expert = seq * 2 + tp
+    lanes = lax.broadcasted_iota(jnp.int32, (1, LANES), 1)
+    picker = jnp.where(lanes == my_expert + first, 256.0 / 65536.0, 0.0)
+    picker += jnp.where(lanes == my_expert + (first + expert_count), 1.0 / 65536.0, 0.0)
+
+    def down_part(activation, which):
+        cols = down_w[pl.ds(pl.multiple_of(which * half_width, 16), half_width), :]
+        return lax.dot_general(
+            activation, cols, (((1,), (1,)), ((), ())), preferred_element_type=jnp.float32
+        )
+
+    def compute(event):
+        x_in[event].wait_recv()
+        to_core(event, 1)
+        if event > 0:
+            p_in[event, 0].wait_recv()
+        p_in[event, 1].wait_recv()
+        block = blocks[event]
+        rows_in = tokens[block]
+        gate_pre = jnp.dot(rows_in, gate_w[...], preferred_element_type=jnp.float32)
+        up_pre = jnp.dot(rows_in, up_w[...], preferred_element_type=jnp.float32)
+        activation = ((up_pre + 1.0) * gate_pre * jax.nn.sigmoid(1.702 * gate_pre)).astype(jnp.bfloat16)
+        share = tokens[block, :, tail:padded].astype(jnp.float32)
+        share = jnp.sum(share * picker, axis=1, keepdims=True)
+        other[event] = (down_part(activation, 1 - tp) * share).astype(jnp.bfloat16)
+        r_in[event] = send(
+            other.at[event], other_in.at[event], rp_send.at[event], rp_recv.at[event], core
+        )
+        mine[event] = down_part(activation, tp) * share
+
+    def join_cores(event):
+        r_in[event].wait_recv()
+        across[event] = (
+            mine[event, rows:, :] + other_in[event, rows:, :].astype(jnp.float32)
+        ).astype(jnp.bfloat16)
+        rx_in[event] = send(
+            across.at[event], across_in.at[event], rx_send.at[event], rx_recv.at[event], side
+        )
+
+    def join_sides(event):
+        rx_in[event].wait_recv()
+        total = mine[event, 0:rows, :] + other_in[event, 0:rows, :].astype(jnp.float32)
+        total += across_in[event].astype(jnp.float32)
+        if event == 0:
+            return total
+        along[event] = total.astype(jnp.bfloat16)
+        send(
+            along.at[event], along_in.at[seq], rz_send.at[event], rz_recv.at[seq],
+            {"seq": blocks[event]},
+        )
+
+    block_across(0)
+    block_along(0, 0, jnp.minimum(seq + 1, last), seq < last)
+    block_along(0, seq_count, jnp.maximum(seq - 1, 0), seq > 0)
+    for event in range(1, min(3, seq_count)):
+        arrive(event)
+    for load in loads:
+        load.wait()
+    compute(0)
+    for event in range(1, seq_count):
+        if event + 2 < seq_count:
+            arrive(event + 2)
+        compute(event)
+        join_cores(event)
+        if event > 1:
+            join_sides(event - 1)
+    join_cores(0)
+    if last > 0:
+        join_sides(last)
+    total = join_sides(0)
+    for event in range(1, seq_count):
+        source = blocks[event]
+        describe(
+            along.at[event], along_in.at[source], rz_send.at[event], rz_recv.at[source], side
+        ).wait_recv()
+        total += along_in[source].astype(jnp.float32)
+    final[:, 0:half_width] = total
+    for low in range(0, half_width, LANES):
+        count = min(LANES, half_width - low)
+        piece = final[:, low : low + LANES].T
+        out_ref[low : low + count, :] = piece[0:count, :].astype(jnp.bfloat16)
+    for copy, parts, when in sends:
+        if when is None:
+            copy.wait_send()
+        else:
+            pl.when(when)(lambda parts=parts: describe(*parts).wait_send())
+
+
+def gathered(hidden, expert_ids, gate_units, w_gate, w_up, w_down):
+    rows, width = hidden.shape
+    units = w_gate.shape[2]
+    seq_count = lax.axis_size("seq")
+    half = width // 2
+    padded = -(-width // LANES) * LANES
+    vmem = pl.BlockSpec(memory_space=pltpu.VMEM)
+    hbm = pl.BlockSpec(memory_space=pl.ANY)
+    dma = pltpu.SemaphoreType.DMA
+    sems = [dma((seq_count,))] * 2
+    return pl.pallas_call(
+        functools.partial(gather_kernel, seq_count),
+        out_shape=jax.ShapeDtypeStruct((half, rows), jnp.bfloat16),
+        in_specs=[vmem] * 3 + [hbm] * 3,
+        out_specs=vmem,
+        scratch_shapes=[
+            pltpu.VMEM((seq_count, 2 * rows, padded), jnp.bfloat16),
+            pltpu.VMEM((padded, units), jnp.bfloat16),
+            pltpu.VMEM((padded, units), jnp.bfloat16),
+            pltpu.VMEM((width, units), jnp.bfloat16),
+            pltpu.VMEM((seq_count, 2 * rows, half), jnp.float32),
+            pltpu.VMEM((seq_count, 2 * rows, half), jnp.bfloat16),
+            pltpu.VMEM((seq_count, 2 * rows, half), jnp.bfloat16),
+            pltpu.VMEM((seq_count, rows, half), jnp.bfloat16),
+            pltpu.VMEM((seq_count, rows, half), jnp.bfloat16),
+            pltpu.VMEM((seq_count, rows, half), jnp.bfloat16),
+            pltpu.VMEM((seq_count, rows, half), jnp.bfloat16),
+            pltpu.VMEM((rows, -(-half // LANES) * LANES), jnp.float32),
+            dma((3,)),
+        ]
+        + sems * 4
+        + [dma((2 * seq_count,))] * 2
+        + [dma((seq_count + 1,)), dma((seq_count,))],
+        compiler_params=pltpu.CompilerParams(
+            collective_id=0, has_side_effects=True, vmem_limit_bytes=60 * 1024 * 1024
+        ),
+    )(hidden.T, expert_ids.T, gate_units.T, w_gate, w_up, w_down).T
+
+
+def local(hidden, expert_ids, gate_units, w_gate, w_up, w_down):
+    token_count, model_width = hidden.shape
+    seq_count = lax.axis_size("seq")
+    expert_count = seq_count * lax.axis_size("tp")
+    spare = -model_width % LANES
+    pairs = lax.axis_size("ep") == 2 and lax.axis_size("tp") == 2
+    whole_blocks = 2 * token_count * TOP * 11 >= expert_count * 8 * token_count
+    if pairs and whole_blocks and 2 * expert_count <= spare:
+        return gathered(hidden, expert_ids, gate_units, w_gate, w_up, w_down)
+    return routed(hidden, expert_ids, gate_units, w_gate, w_up, w_down)
+
+
 def solution(mesh):
     return jax.shard_map(
         local,

time: 158 us -> 55.2 us (0.35)
  blocking collectives: 67.5 us -> 0 us
  Pallas kernels: 0 us -> 53.4 us
  waiting for transfers between devices: 48.5 us -> 0 us
  matrix products: 15.2 us -> 0 us
  local copies, waits for them, and re-layouts: 14.1 us -> 1.61 us
  other arithmetic: 7.45 us -> 0 us
  starting transfers between devices: 4.5 us -> 0 us
    all_to_all x2 -> x0, blocking collectives: 67.5 us -> none  [the longest x1 57.4 us: local(): lax.all_to_all(copied, ('seq', 'ep'), split_axis=0, concat_axis=0, tiled=...]
    pallas_call x0 -> x1, Pallas kernels: none -> 53.4 us  [gathered(): pl.pallas_call(functools.partial(gather_kernel, seq_count), out_shape=jax...]
    all_to_all x1 -> x0, waiting for transfers between devices: 48.5 us -> none  [local(): lax.all_to_all(slice_rows, ('seq', 'ep'), split_axis=0, concat_axis=0, ti...]
    dot_general x4 -> x0, matrix products: 15.2 us -> none  [the longest x1 8.55 us: slice_output(): lax.dot_general(activation, down_cols, (((1,), (1,)), ((), ())), preferre...]
    all_to_all x2 -> x0, local copies, waits for them, and re-layouts: 10.9 us -> none  [the longest x1 6.16 us: local(): lax.all_to_all(lax.all_to_all(slice_rows, ('seq', 'ep'), split_axis=0, co...]
    reduce_sum x3 -> x0, other arithmetic: 5.46 us -> none  [the longest x1 5.2 us: local(): jnp.sum(came_back.astype(jnp.float32), axis=2).astype(jnp.bfloat16)]
    all_to_all x1 -> x0, starting transfers between devices: 4.5 us -> none  [local(): lax.all_to_all(slice_rows, ('seq', 'ep'), split_axis=0, concat_axis=0, ti...]
  transfers between devices with their start and end apart: 1 -> 0, of which waited for: 1 -> 0; matrix products, arithmetic and copies ran while one was open for 0% -> 0% of each run, Pallas kernels for 0% -> 0%
where the time goes in v2:
time: 55.2 us; the launch traced here: 55 us
  Pallas kernels  53.4 us (97%)
  local copies, waits for them, and re-layouts  1.61 us (3%)
    pallas_call x1, Pallas kernels, gathered(): pl.pallas_call(functools.partial(gather_kernel, seq_count), out_shape=jax...  53.4 us
    unnamed x1, local copies, waits for them, and re-layouts  1.61 us

profile of v2, /device:TPU:0, one launch (start us, length us, event | category | flops | bytes accessed | tf_op | source)
XLA Modules:
  0.0 55.0 jit_solution(3252814531436479075)
XLA Ops:
  0.0 53.4 %shard_map.64 = bf16[720,128]{1,0:T(8,128)(2,1)} custom-call(bf16[1440,128]{1,0:T(8,128)(2,1)} %bitcast.5, s32[4,128]{1,0:T(4,128)} %bitcast.6, s32[4,128]{1,0:T(4,128)} %bitcast.7, bf16[1,1440,720]{2,1,0:T(8,128)(2,1)} %gate_hbm.1, bf16[1,1440,720]{2,1,0:T(8,128)(2,1)} %up_hbm.1, bf16[1,1440,720]{2,1,0:T(8,128)(2,1)} %down_hbm.1), custom_call_target="tpu_custom_call" | custom-call | tf_op jit(solution)/shard_map/pallas_call | solution.py:286
  53.4 1.6 %copy.8 = bf16[128,720]{0,1:T(8,128)(2,1)} copy(bf16[128,720]{0,1:T(8,128)(2,1)} %bitcast.4) | data formatting | bytes 368640

commit v3 on v2

--- a/solution.py
+++ b/solution.py
@@ -74,7 +74,7 @@
 
 def gather_kernel(
     seq_count, hidden_ref, ids_ref, units_ref, gate_hbm, up_hbm, down_hbm, out_ref,
-    tokens, gate_w, up_w, down_w, mine, other, other_in, across, across_in, along, along_in, final,
+    tokens, gate_w, up_w, down_w, mine, other, other_in, across, across_in, along, along_in,
     load_sem, gx_send, gx_recv, rp_send, rp_recv, rx_send, rx_recv, rz_send, rz_recv,
     gp_send, gp_recv, gz_send, gz_recv,
 ):
@@ -186,14 +186,14 @@
         to_core(event, 0)
 
     my_expert = seq * 2 + tp
-    lanes = lax.broadcasted_iota(jnp.int32, (1, LANES), 1)
+    lanes = lax.broadcasted_iota(jnp.int32, (LANES, 1), 0)
     picker = jnp.where(lanes == my_expert + first, 256.0 / 65536.0, 0.0)
     picker += jnp.where(lanes == my_expert + (first + expert_count), 1.0 / 65536.0, 0.0)
 
     def down_part(activation, which):
         cols = down_w[pl.ds(pl.multiple_of(which * half_width, 16), half_width), :]
         return lax.dot_general(
-            activation, cols, (((1,), (1,)), ((), ())), preferred_element_type=jnp.float32
+            cols, activation, (((1,), (1,)), ((), ())), preferred_element_type=jnp.float32
         )
 
     def compute(event):
@@ -207,8 +207,8 @@
         gate_pre = jnp.dot(rows_in, gate_w[...], preferred_element_type=jnp.float32)
         up_pre = jnp.dot(rows_in, up_w[...], preferred_element_type=jnp.float32)
         activation = ((up_pre + 1.0) * gate_pre * jax.nn.sigmoid(1.702 * gate_pre)).astype(jnp.bfloat16)
-        share = tokens[block, :, tail:padded].astype(jnp.float32)
-        share = jnp.sum(share * picker, axis=1, keepdims=True)
+        share = tokens[block, :, tail:padded].astype(jnp.float32).T
+        share = jnp.sum(share * picker, axis=0, keepdims=True)
         other[event] = (down_part(activation, 1 - tp) * share).astype(jnp.bfloat16)
         r_in[event] = send(
             other.at[event], other_in.at[event], rp_send.at[event], rp_recv.at[event], core
@@ -218,7 +218,7 @@
     def join_cores(event):
         r_in[event].wait_recv()
         across[event] = (
-            mine[event, rows:, :] + other_in[event, rows:, :].astype(jnp.float32)
+            mine[event, :, rows:] + other_in[event, :, rows:].astype(jnp.float32)
         ).astype(jnp.bfloat16)
         rx_in[event] = send(
             across.at[event], across_in.at[event], rx_send.at[event], rx_recv.at[event], side
@@ -226,7 +226,7 @@
 
     def join_sides(event):
         rx_in[event].wait_recv()
-        total = mine[event, 0:rows, :] + other_in[event, 0:rows, :].astype(jnp.float32)
+        total = mine[event, :, 0:rows] + other_in[event, :, 0:rows].astype(jnp.float32)
         total += across_in[event].astype(jnp.float32)
         if event == 0:
             return total
@@ -261,11 +261,7 @@
             along.at[event], along_in.at[source], rz_send.at[event], rz_recv.at[source], side
         ).wait_recv()
         total += along_in[source].astype(jnp.float32)
-    final[:, 0:half_width] = total
-    for low in range(0, half_width, LANES):
-        count = min(LANES, half_width - low)
-        piece = final[:, low : low + LANES].T
-        out_ref[low : low + count, :] = piece[0:count, :].astype(jnp.bfloat16)
+    out_ref[...] = total.astype(jnp.bfloat16)
     for copy, parts, when in sends:
         if when is None:
             copy.wait_send()
@@ -293,14 +289,13 @@
             pltpu.VMEM((padded, units), jnp.bfloat16),
             pltpu.VMEM((padded, units), jnp.bfloat16),
             pltpu.VMEM((width, units), jnp.bfloat16),
-            pltpu.VMEM((seq_count, 2 * rows, half), jnp.float32),
-            pltpu.VMEM((seq_count, 2 * rows, half), jnp.bfloat16),
-            pltpu.VMEM((seq_count, 2 * rows, half), jnp.bfloat16),
-            pltpu.VMEM((seq_count, rows, half), jnp.bfloat16),
-            pltpu.VMEM((seq_count, rows, half), jnp.bfloat16),
-            pltpu.VMEM((seq_count, rows, half), jnp.bfloat16),
-            pltpu.VMEM((seq_count, rows, half), jnp.bfloat16),
-            pltpu.VMEM((rows, -(-half // LANES) * LANES), jnp.float32),
+            pltpu.VMEM((seq_count, half, 2 * rows), jnp.float32),
+            pltpu.VMEM((seq_count, half, 2 * rows), jnp.bfloat16),
+            pltpu.VMEM((seq_count, half, 2 * rows), jnp.bfloat16),
+            pltpu.VMEM((seq_count, half, rows), jnp.bfloat16),
+            pltpu.VMEM((seq_count, half, rows), jnp.bfloat16),
+            pltpu.VMEM((seq_count, half, rows), jnp.bfloat16),
+            pltpu.VMEM((seq_count, half, rows), jnp.bfloat16),
             dma((3,)),
         ]
         + sems * 4

time: 55.2 us -> 54.7 us (level)
  no operation moved by 1% of the time
where the time goes in v3:
time: 54.7 us; the launch traced here: 54.5 us
  Pallas kernels  52.9 us (97%)
  local copies, waits for them, and re-layouts  1.61 us (3%)
    pallas_call x1, Pallas kernels, gathered(): pl.pallas_call(functools.partial(gather_kernel, seq_count), out_shape=jax...  52.9 us
    unnamed x1, local copies, waits for them, and re-layouts  1.61 us

profile of v3, /device:TPU:0, one launch (start us, length us, event | category | flops | bytes accessed | tf_op | source)
XLA Modules:
  0.0 54.5 jit_solution(4574701745271703285)
XLA Ops:
  0.0 52.9 %shard_map.64 = bf16[720,128]{1,0:T(8,128)(2,1)} custom-call(bf16[1440,128]{1,0:T(8,128)(2,1)} %bitcast.5, s32[4,128]{1,0:T(4,128)} %bitcast.6, s32[4,128]{1,0:T(4,128)} %bitcast.7, bf16[1,1440,720]{2,1,0:T(8,128)(2,1)} %gate_hbm.1, bf16[1,1440,720]{2,1,0:T(8,128)(2,1)} %up_hbm.1, bf16[1,1440,720]{2,1,0:T(8,128)(2,1)} %down_hbm.1), custom_call_target="tpu_custom_call" | custom-call | tf_op jit(solution)/shard_map/pallas_call | solution.py:282
  52.9 1.6 %copy.8 = bf16[128,720]{0,1:T(8,128)(2,1)} copy(bf16[128,720]{0,1:T(8,128)(2,1)} %bitcast.4) | data formatting | bytes 368640
